TPU v7x, 256 devices: a whole 4x4x8 slice. The times are simulated.
256 devices in a mesh: tile: 32 (over z, x_hi, core), group: 8 (over y, x_lo).
Axes of the slice: x: 4 (x_hi: 2, x_lo: 2; x = x_hi * 2 + x_lo), y: 4, z: 8, core: 2. Of those that a mesh axis runs over, the one named last changes fastest.
Arguments:
- object_field: float32 [2, 320, 4096], P(None, 'group', 'tile'), may hold values from -6 to 6
- probe_field: float32 [2, 256, 256], replicated, may hold values from -6 to 6
- amplitudes: float32 [256, 256, 256], P(('tile', 'group')), may hold values from 0 to 4
- row_start: int32 [256], P(('tile', 'group')), may hold values from 0 to 64
- column_start: int32 [256], P(('tile', 'group')), may hold values from 0 to 128
- live_slots: int32 [256], P(('tile', 'group')), may hold values 0 or 1
Outputs:
- new_object: float32 [2, 320, 4096], P(None, 'group', 'tile')
- new_probe: float32 [2, 256, 256], replicated
All inputs are finite; a program needn't handle non-finite values. No bound on the sum of `live_slots` on one device may be relied on, other than what follows from the above.
Results may differ from a plain program's by a relative error of at most 0.0001.
Values sent between devices are 32-bit elements; how exact they have to be, the bound alone decides.
No kernel may reach another device: no remote copies, remote signals or barrier semaphores. Data moves between devices by JAX's collectives and lax.ppermute only.
A program may use at most 64 MiB of HBM per device.

v0:
```python
import math
import jax
import jax.numpy as jnp
from jax import lax
from jax.sharding import PartitionSpec as P

WIN = 256
HALO = 128


def padded_2(value, sides, width):
    for axis, dim in sides:
        count, length = (lax.axis_size(axis), value.shape[dim])
        up = [(i, (i + 1) % count) for i in range(count - 1)]
        down = [(j, i) for i, j in up]
        last = lax.slice_in_dim(value, length - width, length, axis=dim)
        initial = lax.slice_in_dim(value, 0, width, axis=dim)
        before = lax.ppermute(last, axis, up)
        after = lax.ppermute(initial, axis, down)
        value = jnp.concatenate([before, value, after], axis=dim)
    return value


def dft_tables(length):
    counter = jnp.arange(length, dtype=jnp.int32)
    product = counter[:, None] * counter[None, :] % length
    angles = 2.0 * math.pi / length * product.astype(jnp.float32)
    factor = 1.0 / math.sqrt(length)
    return (jnp.cos(angles) * factor, jnp.sin(angles) * factor)


def apply_left(matrix, values):
    return jnp.einsum("jk,pkl->pjl", matrix, values, precision=lax.Precision.HIGHEST)


def apply_right(values, matrix):
    return jnp.einsum("pjk,kl->pjl", values, matrix, precision=lax.Precision.HIGHEST)


def transform(real_part, imag_part, cos_table, sin_table, sign):
    left_real = apply_left(cos_table, real_part) - sign * apply_left(sin_table, imag_part)
    left_imag = apply_left(cos_table, imag_part) + sign * apply_left(sin_table, real_part)
    right_real = apply_right(left_real, cos_table) - sign * apply_right(left_imag, sin_table)
    right_imag = apply_right(left_imag, cos_table) + sign * apply_right(left_real, sin_table)
    return (right_real, right_imag)


def window_terms(windows, probe_field, amplitudes, live_slots, cos_table, sin_table):
    sample_real = windows[:, 0]
    sample_imag = windows[:, 1]
    probe_real = probe_field[0]
    probe_imag = probe_field[1]
    exit_real = probe_real * sample_real - probe_imag * sample_imag
    exit_imag = probe_real * sample_imag + probe_imag * sample_real
    far_real, far_imag = transform(exit_real, exit_imag, cos_table, sin_table, -1.0)
    modulus = jnp.maximum(jnp.sqrt(far_real * far_real + far_imag * far_imag), 0.25)
    factor = 1.0 - amplitudes / modulus
    miss_real, miss_imag = transform(
        far_real * factor, far_imag * factor, cos_table, sin_table, 1.0
    )
    weight = live_slots.astype(jnp.float32)[:, None, None]
    miss_real = miss_real * weight
    miss_imag = miss_imag * weight
    grad_real = probe_real * miss_real + probe_imag * miss_imag
    grad_imag = probe_real * miss_imag - probe_imag * miss_real
    probe_light = weight * (probe_real * probe_real + probe_imag * probe_imag)
    terms = jnp.stack([grad_real, grad_imag, probe_light], axis=1)
    probe_grad = jnp.stack(
        [
            jnp.sum(sample_real * miss_real + sample_imag * miss_imag, axis=0),
            jnp.sum(sample_real * miss_imag - sample_imag * miss_real, axis=0),
        ],
        axis=0,
    )
    window_light = jnp.sum(weight * (sample_real * sample_real + sample_imag * sample_imag), axis=0)
    return (terms, probe_grad, window_light)


def add_windows(accum, terms, top_rows, left_edges):
    zero_index = jnp.zeros((), jnp.int32)
    channels = terms.shape[1]

    def place(slot, current):
        corner = (zero_index, top_rows[slot], left_edges[slot])
        piece = lax.dynamic_slice(current, corner, (channels, WIN, WIN))
        return lax.dynamic_update_slice(current, piece + terms[slot], corner)

    return lax.fori_loop(0, terms.shape[0], place, accum)


def cut_windows(padded, top_rows, left_edges):
    zero_index = jnp.zeros((), jnp.int32)

    def single(top_row, left_edge):
        return lax.dynamic_slice(padded, (zero_index, top_row, left_edge), (2, WIN, WIN))

    return jax.vmap(single)(top_rows, left_edges)


def edge_strips(accum):
    return jnp.concatenate([accum[:, :, :HALO], accum[:, :, accum.shape[2] - HALO :]], axis=2)


def add_edges(inner, arrived):
    width = inner.shape[2]
    inner = inner.at[:, :, :HALO].add(arrived[:, :, :HALO])
    return inner.at[:, :, width - HALO :].add(arrived[:, :, arrived.shape[2] - HALO :])


def apply_updates(object_field, probe_field, share, probe_grad, window_light):
    light_max = jnp.max(probe_field[0] * probe_field[0] + probe_field[1] * probe_field[1]) + 1e-06
    new_object = object_field - share[0:2] / (share[2:3] + 0.25 * light_max)
    new_probe = (
        probe_field - probe_grad / (window_light + 0.25 * jnp.mean(window_light) + 1e-05)[None]
    )
    return (new_object, new_probe)


def local(object_field, probe_field, amplitudes, row_start, column_start, live_slots):
    cos_table, sin_table = dft_tables(WIN)
    full_rows = lax.all_gather(object_field, "group", axis=1, tiled=True)
    padded = padded_2(full_rows, (("tile", 2),), HALO)
    windows = cut_windows(padded, row_start, column_start)
    terms, probe_grad, window_light = window_terms(
        windows, probe_field, amplitudes, live_slots, cos_table, sin_table
    )
    accum = jnp.zeros((terms.shape[1], padded.shape[1], padded.shape[2]), jnp.float32)
    accum = add_windows(accum, terms, row_start, column_start)
    arrived = padded_2(edge_strips(accum), (("tile", 2),), HALO)
    summed = add_edges(accum[:, :, HALO : accum.shape[2] - HALO], arrived)
    share = lax.psum_scatter(summed, "group", scatter_dimension=1, tiled=True)
    probe_grad, window_light = lax.psum((probe_grad, window_light), ("tile", "group"))
    object_field, probe_field = apply_updates(
        object_field, probe_field, share, probe_grad, window_light
    )
    return (object_field, probe_field)


def solution(mesh):
    return jax.shard_map(
        local,
        mesh=mesh,
        in_specs=(
            P(None, "group", "tile"),
            P(),
            P(("tile", "group"), None, None),
            P(("tile", "group")),
            P(("tile", "group")),
            P(("tile", "group")),
        ),
        out_specs=(P(None, "group", "tile"), P()),
        check_vma=False,
    )
```

profile of v0, /device:TPU:2, one launch (start us, length us, event | category | flops | bytes accessed | tf_op | source)
XLA Modules:
  0.0 370.7 jit_solution(3378128131235949026)
XLA Ops:
  8.1 29.8 %all_gather.3 = f32[2,320,128]{2,1,0:T(8,128)S(1)} all-gather(f32[2,40,128]{2,1,0:T(8,128)} %param.14), channel_id=1, replica_groups=mesh['tile'=32,'group'=8] {'group'}, dimensions={1}, use_global_device_ids=true | all-gather | bytes 368640 | tf_op jit(solution)/shard_map/all_gather | solution.py:121
  37.9 1.3 collective-permute-start.1
  39.2 3.1 collective-permute-start
  44.7 1.5 fusion.38
  46.2 1.5 fusion.34
  47.7 1.5 fusion.9
  49.2 1.5 fusion.7
  50.7 1.5 fusion.47
  52.2 1.5 fusion.48
  53.6 1.5 fusion.4
  55.1 1.7 bitcast_multiply_fusion.11
  56.9 1.5 fusion.31
  58.4 1.5 fusion.27
  59.8 1.5 fusion.3
  61.3 1.5 fusion.2
  62.8 1.5 fusion.45
  64.3 1.5 fusion.46
  65.8 1.5 fusion
  67.3 1.7 fusion.1
  69.9 10.9 %dynamic_update_slice.4 = f32[3,320,384]{2,1,0:T(8,128)S(1)} dynamic-update-slice(f32[3,320,384]{2,1,0:T(8,128)S(1)} %broadcast_in_dim.6, f32[3,256,256]{2,1,0:T(8,128)S(1)} %maximum_bitcast_fusion, s32[]{:T(128)} %constant.112.clone.1, s32[]{:T(128)S(6)} %select_n.60, s32[]{:T(128)S(6)} %select_n.61) | dynamic-update-slice | bytes 1572868 | tf_op jit(solution)/shard_map/while/body/eval_jaxpr/dynamic_update_slice | solution.py:86
  80.8 0.9 fusion.132
  81.6 6.6 %collective-permute-start.2 = (f32[3,320,128]{2,1,0:T(8,128)}, f32[3,320,128]{2,1,0:T(8,128)S(1)}, u32[]{:S(2)}, u32[]{:S(2)}) collective-permute-start(f32[3,320,128]{2,1,0:T(8,128)} %get-tuple-element.73), channel_id=1, source_target_pairs={{0,8},{8,16},{16,24},{24,32},{32,40},{40,48},{48,56},{56,64},{64,7... | collective-permute-start | bytes 1474568 | tf_op jit(solution)/shard_map/ppermute | solution.py:18
  88.2 1.3 collective-permute-start.3
  89.6 0.8 fusion.18
  90.4 0.8 pad_maximum_fusion
  91.3 4.5 %collective-permute-done.3 = f32[3,320,128]{2,1,0:T(8,128)} collective-permute-done((f32[3,320,128]{2,1,0:T(8,128)S(1)}, f32[3,320,128]{2,1,0:T(8,128)}, u32[]{:S(2)}, u32[]{:S(2)}) %collective-permute-start.3) | collective-permute-done | bytes 491552 | tf_op jit(solution)/shard_map/ppermute | solution.py:19
  95.7 1.9 fusion.13
  98.3 257.6 %all-reduce.3.cloned.1.call-done = (f32[2,256,256]{2,1,0:T(8,128)}, f32[256,256]{1,0:T(8,128)}) async-done(((f32[2,256,256]{2,1,0:T(8,128)}, f32[256,256]{1,0:T(8,128)}), (f32[2,256,256]{2,1,0:T(8,128)}, f32[256,256]{1,0:T(8,128)})) %all-reduce.3.cloned.1.call-update) | async-done | bytes 786448 | tf_op jit(solution)/shard_map/psum | solution.py:132
  355.9 1.6 reduce_sum.8
  358.2 1.0 add_add_fusion
  359.2 1.9 divide_subtract_fusion
  361.9 1.4 fusion.50
  (28 shorter events, 2.2 us)
Async XLA Ops:
  8.0 36.6 %copy-start = (f32[2,256,256]{2,1,0:T(8,128)S(1)}, f32[2,256,256]{2,1,0:T(8,128)}, u32[]{:S(2)}) copy-start(f32[2,256,256]{2,1,0:T(8,128)} %param.15) | copy-start | bytes 1572868
  8.0 347.9 %all-reduce.3.cloned.1.call-start = ((), (), s32[]{:S(2)}) async-start(), calls=%async_computation.2 | async-start | bytes 1572864 | tf_op jit(solution)/shard_map/psum | solution.py:132
  37.9 6.3 %collective-permute-start.1 = (f32[2,320,128]{2,1,0:T(8,128)S(1)}, f32[2,320,128]{2,1,0:T(8,128)S(1)}, u32[]{:S(2)}, u32[]{:S(2)}) collective-permute-start(f32[2,320,128]{2,1,0:T(8,128)S(1)} %all_gather.3), channel_id=1, source_target_pairs={{8,0},{16,8},{24,16},{32,24},{40,32},{48,40},{56,48},{64,56},{72,6... | collective-permute-start | bytes 983048 | tf_op jit(solution)/shard_map/ppermute | solution.py:19
  39.2 5.0 %collective-permute-start = (f32[2,320,128]{2,1,0:T(8,128)S(1)}, f32[2,320,128]{2,1,0:T(8,128)S(1)}, u32[]{:S(2)}, u32[]{:S(2)}) collective-permute-start(f32[2,320,128]{2,1,0:T(8,128)S(1)} %all_gather.3), channel_id=1, source_target_pairs={{0,8},{8,16},{16,24},{24,32},{32,40},{40,48},{48,56},{56,64},{64,7... | collective-permute-start | bytes 983048 | tf_op jit(solution)/shard_map/ppermute | solution.py:18
  52.1 3.0 copy-start.6
  67.3 2.4 copy-start.1
  69.0 0.8 copy-start.3
  80.8 8.8 %copy-start.2 = (f32[256,256]{1,0:T(8,128)S(1)}, f32[256,256]{1,0:T(8,128)}, u32[]{:S(2)}) copy-start(f32[256,256]{1,0:T(8,128)} %copy-done.1) | copy-start | bytes 786436
  80.8 8.8 %copy-start.4 = (f32[256,256]{1,0:T(8,128)S(1)}, f32[256,256]{1,0:T(8,128)}, u32[]{:S(2)}) copy-start(f32[256,256]{1,0:T(8,128)} %copy-done.3) | copy-start | bytes 786436
  81.6 9.6 %collective-permute-start.2 = (f32[3,320,128]{2,1,0:T(8,128)}, f32[3,320,128]{2,1,0:T(8,128)S(1)}, u32[]{:S(2)}, u32[]{:S(2)}) collective-permute-start(f32[3,320,128]{2,1,0:T(8,128)} %get-tuple-element.73), channel_id=1, source_target_pairs={{0,8},{8,16},{16,24},{24,32},{32,40},{40,48},{48,56},{56,64},{64,7... | collective-permute-start | bytes 1474568 | tf_op jit(solution)/shard_map/ppermute | solution.py:18
  88.2 7.5 %collective-permute-start.3 = (f32[3,320,128]{2,1,0:T(8,128)S(1)}, f32[3,320,128]{2,1,0:T(8,128)}, u32[]{:S(2)}, u32[]{:S(2)}) collective-permute-start(f32[3,320,128]{2,1,0:T(8,128)S(1)} %get-tuple-element.74), channel_id=1, source_target_pairs={{8,0},{16,8},{24,16},{32,24},{40,32},{48,40},{56,48},{64,56},{72,6... | collective-permute-start | bytes 1474568 | tf_op jit(solution)/shard_map/ppermute | solution.py:19
  91.2 269.9 %reduce-scatter.2.cloned.1.call-start = ((), (), s32[]{:S(2)}) async-start(), calls=%async_computation.1 | async-start | bytes 552960 | tf_op jit(solution)/shard_map/reduce_scatter | solution.py:131
  97.6 264.2 %copy-start.5 = (f32[2,40,128]{2,1,0:T(8,128)S(1)}, f32[2,40,128]{2,1,0:T(8,128)}, u32[]{:S(2)}) copy-start(f32[2,40,128]{2,1,0:T(8,128)} %param.14) | copy-start | bytes 122884
Sparse Core Ops, SparseCore 0:
  91.3 264.5 all-reduce.2
Sparse Core Ops, SparseCore 1:
  97.8 51.0 reduce-scatter.1
where the time goes:
time: 371 us
  waiting for transfers between devices  262 us (71%)
  blocking collectives  29.8 us (8%)
  matrix products  24.1 us (6%)
  between operations  19 us (5%)
  starting transfers between devices  12.3 us (3%)
  local copies, waits for them, and re-layouts  11.9 us (3%)
  other arithmetic  11.4 us (3%)
    psum x1, waiting for transfers between devices, local(): lax.psum((probe_grad, window_light), ('tile', 'group'))  258 us
    all_gather x1, blocking collectives, local(): full_rows = lax.all_gather(object_field, 'group', axis=1, tiled=True)  29.8 us
    dot_general x8, matrix products, apply_right(): jnp.einsum('pjk,kl->pjl', values, matrix, precision=lax.Precision.HIGHEST)  12.3 us
    dot_general x8, matrix products, apply_left(): jnp.einsum('jk,pkl->pjl', matrix, values, precision=lax.Precision.HIGHEST)  11.8 us
    dynamic_update_slice x1, local copies, waits for them, and re-layouts, place(): return lax.dynamic_update_slice(current, piece + terms[slot], corner)  10.9 us
    ppermute x2, starting transfers between devices, padded_2(): before = lax.ppermute(last, axis, up)  9.64 us
  transfers between devices with their start and end apart: 6, of which 2 were waited for; matrix products, arithmetic and copies ran while one was open for 2% of the time, Pallas kernels for 0%

commit v1 on v0

--- a/solution.py
+++ b/solution.py
@@ -6,6 +6,11 @@
 
 WIN = 256
 HALO = 128
+
+
+def one_after_other(array, first, second):
+    partial = lax.psum(array, first)
+    return lax.psum(partial, second)
 
 
 def padded_2(value, sides, width):
@@ -129,7 +134,7 @@
     arrived = padded_2(edge_strips(accum), (("tile", 2),), HALO)
     summed = add_edges(accum[:, :, HALO : accum.shape[2] - HALO], arrived)
     share = lax.psum_scatter(summed, "group", scatter_dimension=1, tiled=True)
-    probe_grad, window_light = lax.psum((probe_grad, window_light), ("tile", "group"))
+    probe_grad, window_light = one_after_other((probe_grad, window_light), "group", "tile")
     object_field, probe_field = apply_updates(
         object_field, probe_field, share, probe_grad, window_light
     )

time: 371 us -> 496 us (1.34)
  waiting for transfers between devices: 262 us -> 389 us
    psum x1 -> x2, waiting for transfers between devices: 258 us -> 342 us  [the longest x1 271 us: one_after_other(): return lax.psum(partial, second)]
    reduce_scatter x1, waiting for transfers between devices: 0.01 us -> 40.7 us  [local(): share = lax.psum_scatter(summed, 'group', scatter_dimension=1, tiled=True)]
  transfers between devices with their start and end apart: 6 -> 7, of which waited for: 2 -> 5; matrix products, arithmetic and copies ran while one was open for 2% -> 3% of each run, Pallas kernels for 0% -> 0%
where the time goes in v1:
time: 496 us; the launch traced here: 494 us
  waiting for transfers between devices  389 us (78%)
  blocking collectives  29.8 us (6%)
  matrix products  24.1 us (5%)
  between operations  17.3 us (3%)
  starting transfers between devices  12.3 us (2%)
  local copies, waits for them, and re-layouts  11.1 us (2%)
  other arithmetic  10.4 us (2%)
    psum x1, waiting for transfers between devices, one_after_other(): return lax.psum(partial, second)  271 us
    psum x1, waiting for transfers between devices, one_after_other(): partial = lax.psum(array, first)  70.8 us
    reduce_scatter x1, waiting for transfers between devices, local(): share = lax.psum_scatter(summed, 'group', scatter_dimension=1, tiled=True)  40.7 us
    all_gather x1, blocking collectives, local(): full_rows = lax.all_gather(object_field, 'group', axis=1, tiled=True)  29.8 us
    dot_general x8, matrix products, apply_right(): jnp.einsum('pjk,kl->pjl', values, matrix, precision=lax.Precision.HIGHEST)  12.3 us
    dot_general x8, matrix products, apply_left(): jnp.einsum('jk,pkl->pjl', matrix, values, precision=lax.Precision.HIGHEST)  11.8 us
    dynamic_update_slice x1, local copies, waits for them, and re-layouts, place(): return lax.dynamic_update_slice(current, piece + terms[slot], corner)  10.9 us
  transfers between devices with their start and end apart: 7, of which 5 were waited for; matrix products, arithmetic and copies ran while one was open for 3% of the time, Pallas kernels for 0%

profile of v1, /device:TPU:2, one launch (start us, length us, event | category | flops | bytes accessed | tf_op | source)
XLA Modules:
  0.0 493.9 jit_solution(9146895240708930813)
XLA Ops:
  7.2 29.8 %all_gather.3 = f32[2,320,128]{2,1,0:T(8,128)S(1)} all-gather(f32[2,40,128]{2,1,0:T(8,128)} %param.14), channel_id=1, replica_groups=mesh['tile'=32,'group'=8] {'group'}, dimensions={1}, use_global_device_ids=true | all-gather | bytes 368640 | tf_op jit(solution)/shard_map/all_gather | solution.py:126
  37.0 1.3 collective-permute-start.1
  38.3 3.1 collective-permute-start
  43.9 1.5 fusion.38
  45.4 1.5 fusion.34
  46.8 1.5 fusion.9
  48.3 1.5 fusion.7
  49.8 1.5 fusion.47
  51.3 1.5 fusion.48
  52.8 1.5 fusion.4
  54.3 1.7 bitcast_multiply_fusion.11
  56.0 1.5 fusion.31
  57.5 1.5 fusion.27
  59.0 1.5 fusion.3
  60.5 1.5 fusion.2
  62.0 1.5 fusion.45
  63.4 1.5 fusion.46
  64.9 1.5 fusion
  66.4 1.7 fusion.1
  69.7 0.8 pad_maximum_fusion
  70.7 10.9 %dynamic_update_slice.4 = f32[3,320,384]{2,1,0:T(8,128)S(1)} dynamic-update-slice(f32[3,320,384]{2,1,0:T(8,128)S(1)} %broadcast_in_dim.6, f32[3,256,256]{2,1,0:T(8,128)S(1)} %maximum_bitcast_fusion, s32[]{:T(128)} %constant.112.clone.1, s32[]{:T(128)S(6)} %select_n.60, s32[]{:T(128)S(6)} %select_n.61) | dynamic-update-slice | bytes 1572868 | tf_op jit(solution)/shard_map/while/body/eval_jaxpr/dynamic_update_slice | solution.py:91
  81.7 6.6 %collective-permute-start.2 = (f32[3,320,128]{2,1,0:T(8,128)S(1)}, f32[3,320,128]{2,1,0:T(8,128)S(1)}, u32[]{:S(2)}, u32[]{:S(2)}) collective-permute-start(f32[3,320,128]{2,1,0:T(8,128)S(1)} %get-tuple-element.75), channel_id=1, source_target_pairs={{0,8},{8,16},{16,24},{24,32},{32,40},{40,48},{48,56},{56,64},{64,7... | collective-permute-start | bytes 1474568 | tf_op jit(solution)/shard_map/ppermute | solution.py:23
  88.3 1.3 collective-permute-start.3
  89.8 5.9 %collective-permute-done.3 = f32[3,320,128]{2,1,0:T(8,128)S(1)} collective-permute-done((f32[3,320,128]{2,1,0:T(8,128)S(1)}, f32[3,320,128]{2,1,0:T(8,128)S(1)}, u32[]{:S(2)}, u32[]{:S(2)}) %collective-permute-start.3) | collective-permute-done | bytes 491552 | tf_op jit(solution)/shard_map/ppermute | solution.py:24
  95.7 0.9 fusion.13
  96.7 70.8 %all-reduce.7.cloned.1.call-done = (f32[2,256,256]{2,1,0:T(8,128)}, f32[256,256]{1,0:T(8,128)}) async-done(((f32[2,256,256]{2,1,0:T(8,128)}, f32[256,256]{1,0:T(8,128)}), (f32[2,256,256]{2,1,0:T(8,128)}, f32[256,256]{1,0:T(8,128)})) %all-reduce.7.cloned.1.call-update) | async-done | bytes 786448 | tf_op jit(solution)/shard_map/psum | solution.py:12
  168.1 40.7 %reduce-scatter.2.cloned.1.call-done = f32[3,40,128]{2,1,0:T(8,128)} async-done(((f32[3,320,128]{2,1,0:T(8,128)}), f32[3,40,128]{2,1,0:T(8,128)}) %reduce-scatter.2.cloned.1.call-update) | async-done | bytes 61456 | tf_op jit(solution)/shard_map/reduce_scatter | solution.py:136
  209.5 1.4 fusion.50
  210.9 271.2 %all-reduce.5.cloned.1.call-done = (f32[2,256,256]{2,1,0:T(8,128)}, f32[256,256]{1,0:T(8,128)}) async-done(((f32[2,256,256]{2,1,0:T(8,128)}, f32[256,256]{1,0:T(8,128)}), (f32[2,256,256]{2,1,0:T(8,128)}, f32[256,256]{1,0:T(8,128)})) %all-reduce.5.cloned.1.call-update) | async-done | bytes 786448 | tf_op jit(solution)/shard_map/psum | solution.py:13
  482.1 1.6 reduce_sum.8
  484.4 1.0 add_add_fusion
  485.4 1.9 divide_subtract_fusion
  (23 shorter events, 3.3 us)
Async XLA Ops:
  7.2 36.6 %copy-start = (f32[2,256,256]{2,1,0:T(8,128)S(1)}, f32[2,256,256]{2,1,0:T(8,128)}, u32[]{:S(2)}) copy-start(f32[2,256,256]{2,1,0:T(8,128)} %param.15) | copy-start | bytes 1572868
  7.2 160.3 %all-reduce.7.cloned.1.call-start = ((), (), s32[]{:S(2)}) async-start(), calls=%async_computation.3 | async-start | bytes 1572864 | tf_op jit(solution)/shard_map/psum | solution.py:12
  37.0 6.3 %collective-permute-start.1 = (f32[2,320,128]{2,1,0:T(8,128)S(1)}, f32[2,320,128]{2,1,0:T(8,128)S(1)}, u32[]{:S(2)}, u32[]{:S(2)}) collective-permute-start(f32[2,320,128]{2,1,0:T(8,128)S(1)} %all_gather.3), channel_id=1, source_target_pairs={{8,0},{16,8},{24,16},{32,24},{40,32},{48,40},{56,48},{64,56},{72,6... | collective-permute-start | bytes 983048 | tf_op jit(solution)/shard_map/ppermute | solution.py:24
  38.3 5.0 %collective-permute-start = (f32[2,320,128]{2,1,0:T(8,128)S(1)}, f32[2,320,128]{2,1,0:T(8,128)S(1)}, u32[]{:S(2)}, u32[]{:S(2)}) collective-permute-start(f32[2,320,128]{2,1,0:T(8,128)S(1)} %all_gather.3), channel_id=1, source_target_pairs={{0,8},{8,16},{16,24},{24,32},{32,40},{40,48},{48,56},{56,64},{64,7... | collective-permute-start | bytes 983048 | tf_op jit(solution)/shard_map/ppermute | solution.py:23
  51.3 3.0 copy-start.2
  70.5 138.3 %reduce-scatter.2.cloned.1.call-start = ((), (), s32[]{:S(2)}) async-start(), calls=%async_computation.1 | async-start | bytes 552960 | tf_op jit(solution)/shard_map/reduce_scatter | solution.py:136
  81.7 8.1 %collective-permute-start.2 = (f32[3,320,128]{2,1,0:T(8,128)S(1)}, f32[3,320,128]{2,1,0:T(8,128)S(1)}, u32[]{:S(2)}, u32[]{:S(2)}) collective-permute-start(f32[3,320,128]{2,1,0:T(8,128)S(1)} %get-tuple-element.75), channel_id=1, source_target_pairs={{0,8},{8,16},{16,24},{24,32},{32,40},{40,48},{48,56},{56,64},{64,7... | collective-permute-start | bytes 1474568 | tf_op jit(solution)/shard_map/ppermute | solution.py:23
  88.3 121.2 %copy-start.1 = (f32[2,40,128]{2,1,0:T(8,128)S(1)}, f32[2,40,128]{2,1,0:T(8,128)}, u32[]{:S(2)}) copy-start(f32[2,40,128]{2,1,0:T(8,128)} %param.14) | copy-start | bytes 122884
  88.3 7.4 %collective-permute-start.3 = (f32[3,320,128]{2,1,0:T(8,128)S(1)}, f32[3,320,128]{2,1,0:T(8,128)S(1)}, u32[]{:S(2)}, u32[]{:S(2)}) collective-permute-start(f32[3,320,128]{2,1,0:T(8,128)S(1)} %get-tuple-element.76), channel_id=1, source_target_pairs={{8,0},{16,8},{24,16},{32,24},{40,32},{48,40},{56,48},{64,56},{72,6... | collective-permute-start | bytes 1474568 | tf_op jit(solution)/shard_map/ppermute | solution.py:24
  96.6 385.5 %all-reduce.5.cloned.1.call-start = ((), (), s32[]{:S(2)}) async-start(), calls=%async_computation.2 | async-start | bytes 1572864 | tf_op jit(solution)/shard_map/psum | solution.py:13
Sparse Core Ops, SparseCore 0:
  70.6 96.7 all-reduce.6
  170.1 38.6 reduce-scatter.1
  211.5 270.6 all-reduce.4
